TPU v7x, 32 devices: a whole 2x2x4 slice. The times are simulated.
32 devices in a mesh: grp: 2 (over y), blk: 4 (over z), sub: 2 (over x), frq: 2 (over core).
Axes of the slice: x: 2, y: 2, z: 4, core: 2. Of those that a mesh axis runs over, the one named last changes fastest.
Arguments:
- spectra: bfloat16 [2, 8192, 4096], P(None, ('grp', 'blk'), ('sub', 'frq')), parts along dimension 1, may hold values from -6 to 6
- channel_mask: int32 [8, 1024], P(('grp', 'blk')), parts along dimension 0, may hold values 0 or 1
- local_channel: int32 [8, 4, 48], P(('grp', 'blk')), parts along dimension 0, may hold values from 0 to 1023
- partner_channel: int32 [8, 4, 48], P(('grp', 'blk')), parts along dimension 0, may hold values from 0 to 31
- stack_owner: int32 [8, 4, 48, 1], P(('grp', 'blk')), parts along dimension 0, may hold values from 0 to 3; in each aligned block of 192 rows (0 to 191, 192 to 383, ..., all dimensions but the last counted through in order) at most 96 rows name the same one
- stack_slot: int32 [8, 4, 48], P(('grp', 'blk')), parts along dimension 0, may hold values from 0 to 31
Outputs:
- stacks: float32 [256, 1024], P(('grp', 'blk'), ('sub', 'frq')), parts along dimension 0
There are 2 independent parts, one for each index of `grp`. A program takes and returns all parts, laid end to end along the dimension named above; each array names one. Nothing has to cross between parts.
Inputs may be any that keep to these rules, and one draw needn't show every extreme that they name: `stack_owner`: of the pairs of one source block, at most 96 name one owner, a bound that some block reaches of them.
All inputs are finite; a program needn't handle non-finite values. No bound on the sum of `channel_mask` on one device may be relied on, other than what follows from the above.
Results may differ from a plain program's by a relative error of at most 0.009.
Values may be sent and summed in bfloat16 or wider, within the bound.
A program may use at most 64 MiB of HBM per device.

v0:
```python
import math
import jax
import jax.numpy as jnp
from jax import lax
from jax.sharding import PartitionSpec as P

NF = 4096
LAGS = 1024
VS_BLK = 32
SLOTS_DEV = 32
CAP = 96


def from_root(block, axis, owner):
    block = jnp.where(lax.axis_index(axis) == owner, block, jnp.zeros_like(block))
    return lax.psum(block, axis)


def lag_rows(first_bin, bin_count):
    bin_index = first_bin + jnp.arange(bin_count, dtype=jnp.int32)
    shifts = jnp.arange(LAGS, dtype=jnp.int32) - LAGS // 2
    phase_angle = jnp.mod(bin_index[:, None] * shifts[None, :], NF).astype(jnp.float32) * (
        2.0 * math.pi / NF
    )
    factor = 1.0 / math.sqrt(NF)
    return jnp.concatenate(
        [jnp.cos(phase_angle) * factor, -jnp.sin(phase_angle) * factor], axis=0
    ).astype(jnp.bfloat16)


def per_device(spectra, channel_mask, local_channel, partner_channel, stack_owner, stack_slot):
    blocks = lax.axis_size("blk")
    bins_here = spectra.shape[2]
    lag_table = lag_rows(lax.axis_index(("sub", "frq")) * bins_here, bins_here)
    masked = spectra * channel_mask[0].astype(jnp.bfloat16)[None, :, None]
    stride_size = masked.shape[1] // VS_BLK
    own_panel = masked.reshape(2, VS_BLK, stride_size, bins_here)[:, :, 0, :]
    local_rows = local_channel[0]
    partner_rows = partner_channel[0]
    pair_step = local_rows.shape[1]
    empty_terms = jnp.zeros((blocks * pair_step, lag_table.shape[1]), jnp.float32)

    def add_pairs(partial_terms, panel_data, source):
        own_pick = lax.dynamic_index_in_dim(local_rows, source, 0, keepdims=False)
        partner_pick = lax.dynamic_index_in_dim(partner_rows, source, 0, keepdims=False)
        own_spectra = jnp.take(masked, own_pick, axis=1).astype(jnp.float32)
        partner_spectra = jnp.take(panel_data, partner_pick, axis=1).astype(jnp.float32)
        real_part = (
            own_spectra[0] * partner_spectra[0] + own_spectra[1] * partner_spectra[1]
        ).astype(jnp.bfloat16)
        imag_part = (
            own_spectra[1] * partner_spectra[0] - own_spectra[0] * partner_spectra[1]
        ).astype(jnp.bfloat16)
        cross_rows = jnp.concatenate([real_part, imag_part], axis=1)
        products = jnp.dot(cross_rows, lag_table, preferred_element_type=jnp.float32)
        start_row = (source * pair_step).astype(jnp.int32)
        return lax.dynamic_update_slice_in_dim(partial_terms, products, start_row, 0)

    def root_turn(turn_index, partial_terms):
        panel_data = from_root(own_panel, "blk", turn_index)
        return add_pairs(partial_terms, panel_data, turn_index)

    partial_terms = lax.fori_loop(0, blocks, root_turn, empty_terms)
    summed = lax.psum_scatter(
        partial_terms.astype(jnp.bfloat16), ("sub", "frq"), scatter_dimension=1, tiled=True
    )
    owners = stack_owner[0].reshape(-1)
    slots_flat = stack_slot[0].reshape(-1)
    lag_width = summed.shape[1]
    owner_hits = (owners[:, None] == jnp.arange(blocks, dtype=jnp.int32)[None, :]).astype(jnp.int32)
    earlier_hits = jnp.cumsum(owner_hits, axis=0) - owner_hits
    bucket_rank = jnp.sum(earlier_hits * owner_hits, axis=1)
    targets = owners * CAP + bucket_rank
    outgoing = jnp.zeros((blocks * CAP, lag_width), jnp.bfloat16).at[targets].set(summed)
    labels = (
        jnp.full((blocks * CAP,), -1.0, jnp.bfloat16)
        .at[targets]
        .set(slots_flat.astype(jnp.bfloat16))
    )
    arrived, arrived_labels = (
        lax.all_to_all(
            outgoing.reshape(blocks, CAP, lag_width), "blk", split_axis=0, concat_axis=0, tiled=True
        ),
        lax.all_to_all(labels.reshape(blocks, CAP), "blk", split_axis=0, concat_axis=0, tiled=True),
    )
    slot_ids = arrived_labels.reshape(-1).astype(jnp.int32)
    selector = (jnp.arange(SLOTS_DEV, dtype=jnp.int32)[:, None] == slot_ids[None, :]).astype(
        jnp.bfloat16
    )
    result_stacks = jnp.dot(
        selector, arrived.reshape(blocks * CAP, lag_width), preferred_element_type=jnp.float32
    )
    return result_stacks


def solution(mesh):
    return jax.shard_map(
        per_device,
        mesh=mesh,
        in_specs=(
            P(None, ("grp", "blk"), ("sub", "frq")),
            P(("grp", "blk"), None),
            P(("grp", "blk"), None, None),
            P(("grp", "blk"), None, None),
            P(("grp", "blk"), None, None, None),
            P(("grp", "blk"), None, None),
        ),
        out_specs=P(("grp", "blk"), ("sub", "frq")),
        check_vma=False,
    )
```

profile of v0, /device:TPU:0, one launch (start us, length us, event | category | flops | bytes accessed | tf_op | source)
XLA Modules:
  0.0 259.1 jit_solution(5674109913671485158)
XLA Ops:
  8.1 2.5 broadcast_multiply_fusion
  10.6 6.2 %copy.30 = bf16[2,1024,1024]{2,0,1:T(2,128)(2,1)} copy(bf16[2,1024,1024]{2,1,0:T(8,128)(2,1)S(1)} %broadcast_multiply_fusion) | data formatting | bytes 8388608 | tf_op jit(solution)/shard_map/while | solution.py:63
  17.3 17.6 %multiply_convert_fusion.1 = (bf16[1024,1024]{1,0:T(8,128)(2,1)S(1)}, bf16[1024,1024]{1,0:T(8,128)(2,1)S(1)}) fusion(s32[1024]{0:T(1024)S(1)} %get-tuple-element.182, s32[1024]{0:T(1024)S(1)} %get-tuple-element.183), kind=kLoop, calls=%fused_computation.40 | loop fusion | flops 19922944 | bytes 4202496 | tf_op jit(solution)/shard_map/convert.4
  34.9 2.4 pad_maximum_fusion
  37.4 176.2 %while.13 = (s32[]{:T(128)}, bf16[192,1024]{1,0:T(8,128)(2,1)S(1)}, s32[4,48]{1,0:T(4,128)S(1)}, bf16[2,1024,1024]{2,0,1:T(2,128)(2,1)}, s32[4,48]{1,0:T(4,128)S...) while((s32[]{:T(128)}, bf16[192,1024]{1,0:T(8,128)(2,1)S(1)}, ...), condition=%wide.region_6.7_spmd, body=%wide.region_4.6_spmd.sunk | while | flops 202640240 | bytes 8989001 | solution.py:63
  38.3 3.1 %gather_fusion.1 = bf16[48,2,1024]{2,1,0:T(2,128)(2,1)S(1)} fusion(bf16[2,1024,1024]{2,0,1:T(2,128)(2,1)} %get-tuple-element.268, s32[1024]{0:T(1024)S(1)} %pad_clamp_fusion.5), kind=kCustom, calls=%fused_computation.clone.1 | custom fusion | bytes 393408 | tf_op jit(solution)/shard_map/while/body/eval_jaxpr/jit(_take)/gather | solution.py:46
  41.7 36.2 %all-reduce.3.cloned.1.call-done = bf16[2,32,1024]{2,0,1:T(2,128)(2,1)} async-done(((bf16[2,32,1024]{2,0,1:T(2,128)(2,1)}), bf16[2,32,1024]{2,0,1:T(2,128)(2,1)}) %all-reduce.3.cloned.1.call-update) | async-done | bytes 131088 | tf_op jit(solution)/shard_map/while/body/eval_jaxpr/psum | solution.py:16
  77.9 1.9 gather_fusion
  80.7 3.0 %convolution_dynamic-update-slice_fusion.2 = bf16[192,1024]{1,0:T(8,128)(2,1)S(1)} fusion(bf16[192,1024]{1,0:T(8,128)(2,1)S(1)} %get-tuple-element.253, s32[]{:T(128)S(6)} %select_n.154, bf16[2048,1024]{1,0:T(8,128)(2,1)} %get-tuple-element.271, bf16[48,1024]{1,0:T(8,128)(2,1)S(1)} %bitcast.61, bf16[48,1024]{1,0:T(8,128)(2,1)S(1)} %bitcast.62), kind=kOutput, calls=%fused_computation.4.clone.1 | convolution fusion | flops 201719808 | bytes 4587524 | tf_op jit(solution)/shard_map/while/body/eval_jaxpr/dot_general | solution.py:55
  84.7 3.1 %gather_fusion.1 = bf16[48,2,1024]{2,1,0:T(2,128)(2,1)S(1)} fusion(bf16[2,1024,1024]{2,0,1:T(2,128)(2,1)} %get-tuple-element.268, s32[1024]{0:T(1024)S(1)} %pad_clamp_fusion.5), kind=kCustom, calls=%fused_computation.clone.1 | custom fusion | bytes 393408 | tf_op jit(solution)/shard_map/while/body/eval_jaxpr/jit(_take)/gather | solution.py:46
  88.1 33.2 %all-reduce.3.cloned.1.call-done = bf16[2,32,1024]{2,0,1:T(2,128)(2,1)} async-done(((bf16[2,32,1024]{2,0,1:T(2,128)(2,1)}), bf16[2,32,1024]{2,0,1:T(2,128)(2,1)}) %all-reduce.3.cloned.1.call-update) | async-done | bytes 131088 | tf_op jit(solution)/shard_map/while/body/eval_jaxpr/psum | solution.py:16
  121.3 1.9 gather_fusion
  124.1 3.0 %convolution_dynamic-update-slice_fusion.2 = bf16[192,1024]{1,0:T(8,128)(2,1)S(1)} fusion(bf16[192,1024]{1,0:T(8,128)(2,1)S(1)} %get-tuple-element.253, s32[]{:T(128)S(6)} %select_n.154, bf16[2048,1024]{1,0:T(8,128)(2,1)} %get-tuple-element.271, bf16[48,1024]{1,0:T(8,128)(2,1)S(1)} %bitcast.61, bf16[48,1024]{1,0:T(8,128)(2,1)S(1)} %bitcast.62), kind=kOutput, calls=%fused_computation.4.clone.1 | convolution fusion | flops 201719808 | bytes 4587524 | tf_op jit(solution)/shard_map/while/body/eval_jaxpr/dot_general | solution.py:55
  128.0 3.1 %gather_fusion.1 = bf16[48,2,1024]{2,1,0:T(2,128)(2,1)S(1)} fusion(bf16[2,1024,1024]{2,0,1:T(2,128)(2,1)} %get-tuple-element.268, s32[1024]{0:T(1024)S(1)} %pad_clamp_fusion.5), kind=kCustom, calls=%fused_computation.clone.1 | custom fusion | bytes 393408 | tf_op jit(solution)/shard_map/while/body/eval_jaxpr/jit(_take)/gather | solution.py:46
  131.5 33.2 %all-reduce.3.cloned.1.call-done = bf16[2,32,1024]{2,0,1:T(2,128)(2,1)} async-done(((bf16[2,32,1024]{2,0,1:T(2,128)(2,1)}), bf16[2,32,1024]{2,0,1:T(2,128)(2,1)}) %all-reduce.3.cloned.1.call-update) | async-done | bytes 131088 | tf_op jit(solution)/shard_map/while/body/eval_jaxpr/psum | solution.py:16
  167.5 3.0 %convolution_dynamic-update-slice_fusion.2 = bf16[192,1024]{1,0:T(8,128)(2,1)S(1)} fusion(bf16[192,1024]{1,0:T(8,128)(2,1)S(1)} %get-tuple-element.253, s32[]{:T(128)S(6)} %select_n.154, bf16[2048,1024]{1,0:T(8,128)(2,1)} %get-tuple-element.271, bf16[48,1024]{1,0:T(8,128)(2,1)S(1)} %bitcast.61, bf16[48,1024]{1,0:T(8,128)(2,1)S(1)} %bitcast.62), kind=kOutput, calls=%fused_computation.4.clone.1 | convolution fusion | flops 201719808 | bytes 4587524 | tf_op jit(solution)/shard_map/while/body/eval_jaxpr/dot_general | solution.py:55
  171.4 3.1 %gather_fusion.1 = bf16[48,2,1024]{2,1,0:T(2,128)(2,1)S(1)} fusion(bf16[2,1024,1024]{2,0,1:T(2,128)(2,1)} %get-tuple-element.268, s32[1024]{0:T(1024)S(1)} %pad_clamp_fusion.5), kind=kCustom, calls=%fused_computation.clone.1 | custom fusion | bytes 393408 | tf_op jit(solution)/shard_map/while/body/eval_jaxpr/jit(_take)/gather | solution.py:46
  174.8 32.9 %all-reduce.3.cloned.1.call-done = bf16[2,32,1024]{2,0,1:T(2,128)(2,1)} async-done(((bf16[2,32,1024]{2,0,1:T(2,128)(2,1)}), bf16[2,32,1024]{2,0,1:T(2,128)(2,1)}) %all-reduce.3.cloned.1.call-update) | async-done | bytes 131088 | tf_op jit(solution)/shard_map/while/body/eval_jaxpr/psum | solution.py:16
  210.5 3.0 %convolution_dynamic-update-slice_fusion.2 = bf16[192,1024]{1,0:T(8,128)(2,1)S(1)} fusion(bf16[192,1024]{1,0:T(8,128)(2,1)S(1)} %get-tuple-element.253, s32[]{:T(128)S(6)} %select_n.154, bf16[2048,1024]{1,0:T(8,128)(2,1)} %get-tuple-element.271, bf16[48,1024]{1,0:T(8,128)(2,1)S(1)} %bitcast.61, bf16[48,1024]{1,0:T(8,128)(2,1)S(1)} %bitcast.62), kind=kOutput, calls=%fused_computation.4.clone.1 | convolution fusion | flops 201719808 | bytes 4587524 | tf_op jit(solution)/shard_map/while/body/eval_jaxpr/dot_general | solution.py:55
  219.9 3.4 %all-to-all-start = ((bf16[4,1,96]{2,1,0:T(2,128)(2,1)}), bf16[4,1,96]{2,1,0:T(2,128)(2,1)S(1)}, u32[]{:S(2)}, u32[]{:S(2)}) async-start(bf16[4,1,96]{2,1,0:T(2,128)(2,1)} %all_to_all.12), calls=%async_computation | async-start | bytes 4096 | tf_op jit(solution)/shard_map/all_to_all | solution.py:84
  223.3 13.7 %reduce-scatter.2.cloned.1.call-done = bf16[192,256]{1,0:T(8,128)(2,1)} async-done(((bf16[192,1024]{1,0:T(8,128)(2,1)}), bf16[192,256]{1,0:T(8,128)(2,1)}) %reduce-scatter.2.cloned.1.call-update) | async-done | bytes 98320 | tf_op jit(solution)/shard_map/reduce_scatter | solution.py:64
  237.0 2.2 scatter_custom_fusion.1
  239.3 4.6 %all-to-all-start.1 = ((bf16[4,96,256]{2,1,0:T(8,128)(2,1)}), bf16[4,96,256]{2,1,0:T(8,128)(2,1)S(1)}, u32[]{:S(2)}, u32[]{:S(2)}) async-start(bf16[4,96,256]{2,1,0:T(8,128)(2,1)} %bitcast.16), calls=%async_computation.2 | async-start | bytes 393216 | tf_op jit(solution)/shard_map/all_to_all | solution.py:81
  244.0 7.2 %all-to-all-done.1 = bf16[4,96,256]{2,1,0:T(8,128)(2,1)S(1)} async-done(((bf16[4,96,256]{2,1,0:T(8,128)(2,1)}), bf16[4,96,256]{2,1,0:T(8,128)(2,1)S(1)}, u32[]{:S(2)}, u32[]{:S(2)}) %all-to-all-start.1) | async-done | bytes 196640 | tf_op jit(solution)/shard_map/all_to_all | solution.py:81
  (92 shorter events, 20.1 us)
Async XLA Ops:
  34.8 2.5 copy-start.1
  34.8 2.5 copy-start.2
  37.3 177.5 %copy-start.4 = (s32[1,4,48,1]{2,3,1,0:T(1,128)S(1)}, s32[1,4,48,1]{2,3,1,0:T(1,128)}, u32[]{:S(2)}) copy-start(s32[1,4,48,1]{2,3,1,0:T(1,128)} %param.12) | copy-start | bytes 2308
  37.3 180.0 %copy-start.3 = (s32[1,4,48]{2,1,0:T(4,128)S(1)}, s32[1,4,48]{2,1,0:T(4,128)}, u32[]{:S(2)}) copy-start(s32[1,4,48]{2,1,0:T(4,128)} %param.13) | copy-start | bytes 2308
  37.4 40.5 %all-reduce.3.cloned.1.call-start = ((), (), s32[]{:S(2)}) async-start(), calls=%async_computation.4 | async-start | bytes 262144 | tf_op jit(solution)/shard_map/while/body/eval_jaxpr/psum | solution.py:16
  83.8 37.5 %all-reduce.3.cloned.1.call-start = ((), (), s32[]{:S(2)}) async-start(), calls=%async_computation.4 | async-start | bytes 262144 | tf_op jit(solution)/shard_map/while/body/eval_jaxpr/psum | solution.py:16
  127.2 37.5 %all-reduce.3.cloned.1.call-start = ((), (), s32[]{:S(2)}) async-start(), calls=%async_computation.4 | async-start | bytes 262144 | tf_op jit(solution)/shard_map/while/body/eval_jaxpr/psum | solution.py:16
  170.5 37.2 %all-reduce.3.cloned.1.call-start = ((), (), s32[]{:S(2)}) async-start(), calls=%async_computation.4 | async-start | bytes 262144 | tf_op jit(solution)/shard_map/while/body/eval_jaxpr/psum | solution.py:16
  213.6 0.7 copy-start
  213.6 23.4 %reduce-scatter.2.cloned.1.call-start = ((), (), s32[]{:S(2)}) async-start(), calls=%async_computation.3 | async-start | bytes 491520 | tf_op jit(solution)/shard_map/reduce_scatter | solution.py:64
  219.9 19.4 %all-to-all-start = ((bf16[4,1,96]{2,1,0:T(2,128)(2,1)}), bf16[4,1,96]{2,1,0:T(2,128)(2,1)S(1)}, u32[]{:S(2)}, u32[]{:S(2)}) async-start(bf16[4,1,96]{2,1,0:T(2,128)(2,1)} %all_to_all.12), calls=%async_computation | async-start | bytes 4096 | tf_op jit(solution)/shard_map/all_to_all | solution.py:84
  239.3 11.9 %all-to-all-start.1 = ((bf16[4,96,256]{2,1,0:T(8,128)(2,1)}), bf16[4,96,256]{2,1,0:T(8,128)(2,1)S(1)}, u32[]{:S(2)}, u32[]{:S(2)}) async-start(bf16[4,96,256]{2,1,0:T(8,128)(2,1)} %bitcast.16), calls=%async_computation.2 | async-start | bytes 393216 | tf_op jit(solution)/shard_map/all_to_all | solution.py:81
Sparse Core Ops, SparseCore 0:
  40.5 37.3 all-reduce.2
  86.9 34.3 all-reduce.2
  130.3 34.3 all-reduce.2
  173.3 34.3 all-reduce.2
Sparse Core Ops, SparseCore 1:
  216.6 20.4 reduce-scatter.1
where the time goes:
time: 260 us; the launch traced here: 259 us
  waiting for transfers between devices  156 us (60%)
  local copies, waits for them, and re-layouts  33.3 us (13%)
  other arithmetic  32.9 us (13%)
  between operations  14.7 us (6%)
  matrix products  12.9 us (5%)
  starting transfers between devices  8.39 us (3%)
    psum x4, waiting for transfers between devices, from_root(): return lax.psum(block, axis)  135 us
    another operation x4, other arithmetic  18.8 us
    reduce_scatter x1, waiting for transfers between devices, per_device(): lax.psum_scatter(partial_terms.astype(jnp.bfloat16), ('sub', 'frq'), scat...  13.7 us
    gather x4, local copies, waits for them, and re-layouts, add_pairs(): own_spectra = jnp.take(masked, own_pick, axis=1).astype(jnp.float32)  12.6 us
    dot_general x4, matrix products, add_pairs(): jnp.dot(cross_rows, lag_table, preferred_element_type=jnp.float32)  12.1 us
    gather x4, local copies, waits for them, and re-layouts, add_pairs(): jnp.take(panel_data, partner_pick, axis=1).astype(jnp.float32)  7.43 us
    all_to_all x1, waiting for transfers between devices, per_device(): lax.all_to_all(outgoing.reshape(blocks, CAP, lag_width), 'blk', split_axi...  7.19 us
    while x2, local copies, waits for them, and re-layouts, per_device(): partial_terms = lax.fori_loop(0, blocks, root_turn, empty_terms)  6.44 us
  transfers between devices with their start and end apart: 7, of which 6 were waited for; matrix products, arithmetic and copies ran while one was open for 8% of the time, Pallas kernels for 0%

commit v1 on v0

--- a/solution.py
+++ b/solution.py
@@ -3,6 +3,7 @@
 import jax.numpy as jnp
 from jax import lax
 from jax.sharding import PartitionSpec as P
+from jax.lax import all_gather
 
 NF = 4096
 LAGS = 1024
@@ -13,7 +14,7 @@
 
 def from_root(block, axis, owner):
     block = jnp.where(lax.axis_index(axis) == owner, block, jnp.zeros_like(block))
-    return lax.psum(block, axis)
+    return jnp.sum(all_gather(block, axis_name=axis), axis=0)
 
 
 def lag_rows(first_bin, bin_count):

time: 260 us -> 181 us (0.70)
  waiting for transfers between devices: 156 us -> 19 us
  blocking collectives: 0 us -> 64 us
  local copies, waits for them, and re-layouts: 33.3 us -> 30.3 us
    psum x4 -> x0, waiting for transfers between devices: 135 us -> none  [from_root(): return lax.psum(block, axis)]
    all_gather x0 -> x4, blocking collectives: none -> 64 us  [from_root(): return jnp.sum(all_gather(block, axis_name=axis), axis=0)]
    gather x4, local copies, waits for them, and re-layouts: 7.43 us -> 3.81 us  [add_pairs(): jnp.take(panel_data, partner_pick, axis=1).astype(jnp.float32)]
    select_n x4, other arithmetic: 2.99 us -> 0.06 us  [from_root(): jnp.where(lax.axis_index(axis) == owner, block, jnp.zeros_like(block))]
    while x2 -> x1, local copies, waits for them, and re-layouts: 6.44 us -> 6.24 us  [per_device(): partial_terms = lax.fori_loop(0, blocks, root_turn, empty_terms)]
  transfers between devices with their start and end apart: 7 -> 3, of which waited for: 6 -> 2; matrix products, arithmetic and copies ran while one was open for 8% -> 4% of each run, Pallas kernels for 0% -> 0%
where the time goes in v1:
time: 181 us; the launch traced here: 180 us
  blocking collectives  64 us (35%)
  other arithmetic  30.4 us (17%)
  local copies, waits for them, and re-layouts  30.3 us (17%)
  waiting for transfers between devices  19 us (10%)
  between operations  13.5 us (7%)
  matrix products  12.9 us (7%)
  starting transfers between devices  9.51 us (5%)
    all_gather x4, blocking collectives, from_root(): return jnp.sum(all_gather(block, axis_name=axis), axis=0)  64 us
    another operation x4, other arithmetic  19 us
    gather x4, local copies, waits for them, and re-layouts, add_pairs(): own_spectra = jnp.take(masked, own_pick, axis=1).astype(jnp.float32)  12.6 us
    dot_general x4, matrix products, add_pairs(): jnp.dot(cross_rows, lag_table, preferred_element_type=jnp.float32)  12.1 us
    reduce_scatter x1, waiting for transfers between devices, per_device(): lax.psum_scatter(partial_terms.astype(jnp.bfloat16), ('sub', 'frq'), scat...  11.8 us
    all_to_all x1, waiting for transfers between devices, per_device(): lax.all_to_all(outgoing.reshape(blocks, CAP, lag_width), 'blk', split_axi...  7.2 us
    while x1, local copies, waits for them, and re-layouts, per_device(): partial_terms = lax.fori_loop(0, blocks, root_turn, empty_terms)  6.24 us
    all_to_all x1, starting transfers between devices, per_device(): lax.all_to_all(labels.reshape(blocks, CAP), 'blk', split_axis=0, concat_a...  4.91 us
  transfers between devices with their start and end apart: 3, of which 2 were waited for; matrix products, arithmetic and copies ran while one was open for 4% of the time, Pallas kernels for 0%

profile of v1, /device:TPU:0, one launch (start us, length us, event | category | flops | bytes accessed | tf_op | source)
XLA Modules:
  0.0 180.1 jit_solution(5382322634119251022)
XLA Ops:
  7.2 2.5 %broadcast_multiply_fusion = bf16[2,1024,1024]{2,1,0:T(8,128)(2,1)S(1)} fusion(bf16[2,1024,1024]{2,1,0:T(8,128)(2,1)} %param.8, bf16[1024]{0:T(1024)(128)(2,1)S(1)} %convert_reduce_fusion), kind=kLoop, calls=%fused_computation.41 | loop fusion | flops 2097152 | bytes 8390656 | tf_op jit(solution)/shard_map/mul | solution.py:36
  9.8 6.2 %copy.28 = bf16[2,1024,1024]{2,0,1:T(2,128)(2,1)} copy(bf16[2,1024,1024]{2,1,0:T(8,128)(2,1)S(1)} %broadcast_multiply_fusion) | data formatting | bytes 8388608 | tf_op jit(solution)/shard_map/while | solution.py:64
  16.3 17.8 %multiply_convert_fusion.1 = (bf16[1024,1024]{1,0:T(8,128)(2,1)S(1)}, bf16[1024,1024]{1,0:T(8,128)(2,1)S(1)}) fusion(s32[1024]{0:T(1024)S(1)} %get-tuple-element.234, s32[1024]{0:T(1024)S(1)} %get-tuple-element.235), kind=kLoop, calls=%fused_computation.40 | loop fusion | flops 19922944 | bytes 4202496 | tf_op jit(solution)/shard_map/convert.9
  34.0 2.4 %pad_maximum_fusion = bf16[2048,1024]{1,0:T(8,128)(2,1)} fusion(bf16[1024,1024]{1,0:T(8,128)(2,1)S(1)} %get-tuple-element.233, bf16[1024,1024]{1,0:T(8,128)(2,1)S(1)} %get-tuple-element.232), kind=kLoop, calls=%fused_computation.38 | loop fusion | flops 8388608 | bytes 8388608 | tf_op jit(solution)/shard_map/concatenate | solution.py:27
  36.6 98.8 %while.15 = (s32[]{:T(128)}, bf16[192,1024]{1,0:T(8,128)(2,1)S(1)}, s32[4,48]{1,0:T(4,128)S(1)}, bf16[2,1024,1024]{2,0,1:T(2,128)(2,1)}, s32[4,48]{1,0:T(4,128)S...) while((s32[]{:T(128)}, bf16[192,1024]{1,0:T(8,128)(2,1)S(1)}, ...), condition=%wide.region_6.7_spmd, body=%wide.region_4.6_spmd.sunk | while | flops 202771312 | bytes 9775403 | solution.py:64
  36.6 17.4 %all-gather.2 = bf16[8,32,1024]{2,1,0:T(8,128)(2,1)S(1)} all-gather(bf16[2,32,1024]{2,1,0:T(8,128)(2,1)S(1)} %broadcast_select_fusion.4), channel_id=2, replica_groups=mesh['grp'=2,'blk'=4,'sub'=2,'frq'=2] {'blk'}, dimensions={0}, use_global_device_ids=true | all-gather | bytes 655360 | tf_op jit(solution)/shard_map/while/body/eval_jaxpr/all_gather | solution.py:17
  55.5 3.1 %gather_fusion.1 = bf16[48,2,1024]{2,1,0:T(2,128)(2,1)S(1)} fusion(bf16[2,1024,1024]{2,0,1:T(2,128)(2,1)} %get-tuple-element.322, s32[1024]{0:T(1024)S(1)} %pad_clamp_fusion.5), kind=kCustom, calls=%fused_computation.clone.1 | custom fusion | bytes 393408 | tf_op jit(solution)/shard_map/while/body/eval_jaxpr/jit(_take)/gather | solution.py:47
  59.6 3.0 %convolution_dynamic-update-slice_fusion.2 = bf16[192,1024]{1,0:T(8,128)(2,1)S(1)} fusion(bf16[192,1024]{1,0:T(8,128)(2,1)S(1)} %get-tuple-element.306, s32[]{:T(128)S(6)} %select_n.189, bf16[2048,1024]{1,0:T(8,128)(2,1)} %get-tuple-element.325, bf16[48,1024]{1,0:T(8,128)(2,1)S(1)} %bitcast.65, bf16[48,1024]{1,0:T(8,128)(2,1)S(1)} %bitcast.66), kind=kOutput, calls=%fused_computation.4.clone.1 | convolution fusion | flops 201719808 | bytes 4587524 | tf_op jit(solution)/shard_map/while/body/eval_jaxpr/dot_general | solution.py:56
  62.7 16.3 %all-gather.2 = bf16[8,32,1024]{2,1,0:T(8,128)(2,1)S(1)} all-gather(bf16[2,32,1024]{2,1,0:T(8,128)(2,1)S(1)} %broadcast_select_fusion.4), channel_id=2, replica_groups=mesh['grp'=2,'blk'=4,'sub'=2,'frq'=2] {'blk'}, dimensions={0}, use_global_device_ids=true | all-gather | bytes 655360 | tf_op jit(solution)/shard_map/while/body/eval_jaxpr/all_gather | solution.py:17
  80.4 3.1 %gather_fusion.1 = bf16[48,2,1024]{2,1,0:T(2,128)(2,1)S(1)} fusion(bf16[2,1024,1024]{2,0,1:T(2,128)(2,1)} %get-tuple-element.322, s32[1024]{0:T(1024)S(1)} %pad_clamp_fusion.5), kind=kCustom, calls=%fused_computation.clone.1 | custom fusion | bytes 393408 | tf_op jit(solution)/shard_map/while/body/eval_jaxpr/jit(_take)/gather | solution.py:47
  84.5 3.0 %convolution_dynamic-update-slice_fusion.2 = bf16[192,1024]{1,0:T(8,128)(2,1)S(1)} fusion(bf16[192,1024]{1,0:T(8,128)(2,1)S(1)} %get-tuple-element.306, s32[]{:T(128)S(6)} %select_n.189, bf16[2048,1024]{1,0:T(8,128)(2,1)} %get-tuple-element.325, bf16[48,1024]{1,0:T(8,128)(2,1)S(1)} %bitcast.65, bf16[48,1024]{1,0:T(8,128)(2,1)S(1)} %bitcast.66), kind=kOutput, calls=%fused_computation.4.clone.1 | convolution fusion | flops 201719808 | bytes 4587524 | tf_op jit(solution)/shard_map/while/body/eval_jaxpr/dot_general | solution.py:56
  87.7 15.6 %all-gather.2 = bf16[8,32,1024]{2,1,0:T(8,128)(2,1)S(1)} all-gather(bf16[2,32,1024]{2,1,0:T(8,128)(2,1)S(1)} %broadcast_select_fusion.4), channel_id=2, replica_groups=mesh['grp'=2,'blk'=4,'sub'=2,'frq'=2] {'blk'}, dimensions={0}, use_global_device_ids=true | all-gather | bytes 655360 | tf_op jit(solution)/shard_map/while/body/eval_jaxpr/all_gather | solution.py:17
  104.7 3.1 %gather_fusion.1 = bf16[48,2,1024]{2,1,0:T(2,128)(2,1)S(1)} fusion(bf16[2,1024,1024]{2,0,1:T(2,128)(2,1)} %get-tuple-element.322, s32[1024]{0:T(1024)S(1)} %pad_clamp_fusion.5), kind=kCustom, calls=%fused_computation.clone.1 | custom fusion | bytes 393408 | tf_op jit(solution)/shard_map/while/body/eval_jaxpr/jit(_take)/gather | solution.py:47
  108.8 3.0 %convolution_dynamic-update-slice_fusion.2 = bf16[192,1024]{1,0:T(8,128)(2,1)S(1)} fusion(bf16[192,1024]{1,0:T(8,128)(2,1)S(1)} %get-tuple-element.306, s32[]{:T(128)S(6)} %select_n.189, bf16[2048,1024]{1,0:T(8,128)(2,1)} %get-tuple-element.325, bf16[48,1024]{1,0:T(8,128)(2,1)S(1)} %bitcast.65, bf16[48,1024]{1,0:T(8,128)(2,1)S(1)} %bitcast.66), kind=kOutput, calls=%fused_computation.4.clone.1 | convolution fusion | flops 201719808 | bytes 4587524 | tf_op jit(solution)/shard_map/while/body/eval_jaxpr/dot_general | solution.py:56
  111.9 14.8 %all-gather.2 = bf16[8,32,1024]{2,1,0:T(8,128)(2,1)S(1)} all-gather(bf16[2,32,1024]{2,1,0:T(8,128)(2,1)S(1)} %broadcast_select_fusion.4), channel_id=2, replica_groups=mesh['grp'=2,'blk'=4,'sub'=2,'frq'=2] {'blk'}, dimensions={0}, use_global_device_ids=true | all-gather | bytes 655360 | tf_op jit(solution)/shard_map/while/body/eval_jaxpr/all_gather | solution.py:17
  128.2 3.1 %gather_fusion.1 = bf16[48,2,1024]{2,1,0:T(2,128)(2,1)S(1)} fusion(bf16[2,1024,1024]{2,0,1:T(2,128)(2,1)} %get-tuple-element.322, s32[1024]{0:T(1024)S(1)} %pad_clamp_fusion.5), kind=kCustom, calls=%fused_computation.clone.1 | custom fusion | bytes 393408 | tf_op jit(solution)/shard_map/while/body/eval_jaxpr/jit(_take)/gather | solution.py:47
  132.3 3.0 %convolution_dynamic-update-slice_fusion.2 = bf16[192,1024]{1,0:T(8,128)(2,1)S(1)} fusion(bf16[192,1024]{1,0:T(8,128)(2,1)S(1)} %get-tuple-element.306, s32[]{:T(128)S(6)} %select_n.189, bf16[2048,1024]{1,0:T(8,128)(2,1)} %get-tuple-element.325, bf16[48,1024]{1,0:T(8,128)(2,1)S(1)} %bitcast.65, bf16[48,1024]{1,0:T(8,128)(2,1)S(1)} %bitcast.66), kind=kOutput, calls=%fused_computation.4.clone.1 | convolution fusion | flops 201719808 | bytes 4587524 | tf_op jit(solution)/shard_map/while/body/eval_jaxpr/dot_general | solution.py:56
  137.4 1.2 reduce-window.6
  139.2 1.8 scatter_custom_fusion
  141.7 4.9 %all-to-all-start = ((bf16[4,1,96]{2,1,0:T(2,128)(2,1)}), bf16[4,1,96]{2,1,0:T(2,128)(2,1)S(1)}, u32[]{:S(2)}, u32[]{:S(2)}) async-start(bf16[4,1,96]{2,1,0:T(2,128)(2,1)} %all_to_all.12), calls=%async_computation | async-start | bytes 4096 | tf_op jit(solution)/shard_map/all_to_all | solution.py:85
  146.6 11.8 %reduce-scatter.2.cloned.1.call-done = bf16[192,256]{1,0:T(8,128)(2,1)} async-done(((bf16[192,1024]{1,0:T(8,128)(2,1)}), bf16[192,256]{1,0:T(8,128)(2,1)}) %reduce-scatter.2.cloned.1.call-update) | async-done | bytes 98320 | tf_op jit(solution)/shard_map/reduce_scatter | solution.py:65
  158.3 2.2 %scatter_custom_fusion.1 = bf16[384,256]{1,0:T(8,128)(2,1)} fusion(s32[192]{0:T(256)S(1)} %bitcast.75, bf16[192,256]{1,0:T(8,128)(2,1)} %reduce-scatter.2.cloned.1.call-done, bf16[]{:T(256)} %constant.195.clone.1), kind=kCustom, calls=%fused_computation.43 | custom fusion | bytes 197120 | tf_op jit(solution)/shard_map/scatter | solution.py:75
  160.6 4.6 %all-to-all-start.1 = ((bf16[4,96,256]{2,1,0:T(8,128)(2,1)}), bf16[4,96,256]{2,1,0:T(8,128)(2,1)S(1)}, u32[]{:S(2)}, u32[]{:S(2)}) async-start(bf16[4,96,256]{2,1,0:T(8,128)(2,1)} %bitcast.16), calls=%async_computation.2 | async-start | bytes 393216 | tf_op jit(solution)/shard_map/all_to_all | solution.py:82
  165.3 7.2 %all-to-all-done.1 = bf16[4,96,256]{2,1,0:T(8,128)(2,1)S(1)} async-done(((bf16[4,96,256]{2,1,0:T(8,128)(2,1)}), bf16[4,96,256]{2,1,0:T(8,128)(2,1)S(1)}, u32[]{:S(2)}, u32[]{:S(2)}) %all-to-all-start.1) | async-done | bytes 196640 | tf_op jit(solution)/shard_map/all_to_all | solution.py:82
  (92 shorter events, 14.8 us)
Async XLA Ops:
  6.5 151.8 %reduce-scatter.2.cloned.1.call-start = ((), (), s32[]{:S(2)}) async-start(), calls=%async_computation.3 | async-start | bytes 491520 | tf_op jit(solution)/shard_map/reduce_scatter | solution.py:65
  34.0 2.5 %copy-start.1 = (s32[1,4,48]{2,1,0:T(4,128)S(1)}, s32[1,4,48]{2,1,0:T(4,128)}, u32[]{:S(2)}) copy-start(s32[1,4,48]{2,1,0:T(4,128)} %param.10) | copy-start | bytes 2308
  34.0 2.5 %copy-start.2 = (s32[1,4,48]{2,1,0:T(4,128)S(1)}, s32[1,4,48]{2,1,0:T(4,128)}, u32[]{:S(2)}) copy-start(s32[1,4,48]{2,1,0:T(4,128)} %param.11) | copy-start | bytes 2308
  36.5 100.1 %copy-start.4 = (s32[1,4,48,1]{2,3,1,0:T(1,128)S(1)}, s32[1,4,48,1]{2,3,1,0:T(1,128)}, u32[]{:S(2)}) copy-start(s32[1,4,48,1]{2,3,1,0:T(1,128)} %param.12) | copy-start | bytes 2308
  36.5 102.6 %copy-start.3 = (s32[1,4,48]{2,1,0:T(4,128)S(1)}, s32[1,4,48]{2,1,0:T(4,128)}, u32[]{:S(2)}) copy-start(s32[1,4,48]{2,1,0:T(4,128)} %param.13) | copy-start | bytes 2308
  135.3 0.7 copy-start
  141.7 18.9 %all-to-all-start = ((bf16[4,1,96]{2,1,0:T(2,128)(2,1)}), bf16[4,1,96]{2,1,0:T(2,128)(2,1)S(1)}, u32[]{:S(2)}, u32[]{:S(2)}) async-start(bf16[4,1,96]{2,1,0:T(2,128)(2,1)} %all_to_all.12), calls=%async_computation | async-start | bytes 4096 | tf_op jit(solution)/shard_map/all_to_all | solution.py:85
  160.6 11.9 %all-to-all-start.1 = ((bf16[4,96,256]{2,1,0:T(8,128)(2,1)}), bf16[4,96,256]{2,1,0:T(8,128)(2,1)S(1)}, u32[]{:S(2)}, u32[]{:S(2)}) async-start(bf16[4,96,256]{2,1,0:T(8,128)(2,1)} %bitcast.16), calls=%async_computation.2 | async-start | bytes 393216 | tf_op jit(solution)/shard_map/all_to_all | solution.py:82
Sparse Core Ops, SparseCore 0:
  136.2 22.0 reduce-scatter.1
